TPU v7x, 512 devices: a whole 4x4x16 slice. The times are simulated.
512 devices in a mesh: src: 64 (over z, x), tm: 8 (over y, core).
Axes of the slice: x: 4, y: 4, z: 16, core: 2. Of those that a mesh axis runs over, the one named last changes fastest.
Arguments:
- left_vector: float32 [8, 131072], P(None, ('src', 'tm')), may hold values from -12 to 12
- source_coeffs: float32 [5, 8, 131072], P(None, None, ('src', 'tm')), may hold values from -1.5 to 1.5
- knot_coeffs: float32 [12, 8, 131072], P(None, None, ('src', 'tm')), may hold values from -1.5 to 1.5
- source_index: int32 [8, 131072], P(None, ('src', 'tm')), may hold values from 0 to 1023
- band_start: int32 [8, 131072], P(None, ('src', 'tm')), may hold values from 0 to 4095, as said below
- bucket_fill: int32 [8, 512], P(None, ('src', 'tm')), may hold values from 51 to 256, as said below
- source_vector: float32 [5, 524288], P(None, ('src', 'tm')), may hold values from -6 to 6
- knot_vector: float32 [3, 8, 16384], P(None, 'tm', 'src'), may hold values from -6 to 6
- source_search: float32 [5, 524288], P(None, ('src', 'tm')), may hold values from -6 to 6
- knot_search: float32 [3, 8, 16384], P(None, 'tm', 'src'), may hold values from -6 to 6
- source_solution: float32 [5, 524288], P(None, ('src', 'tm')), may hold values from -6 to 6
- knot_solution: float32 [3, 8, 16384], P(None, 'tm', 'src'), may hold values from -6 to 6
- recurrence: float32 [3], replicated, may hold values from 0.5 to 1.5
Outputs:
- left_next: float32 [8, 131072], P(None, ('src', 'tm'))
- source_next: float32 [5, 524288], P(None, ('src', 'tm'))
- knot_next: float32 [3, 8, 16384], P(None, 'tm', 'src')
- search_source: float32 [5, 524288], P(None, ('src', 'tm'))
- search_knot: float32 [3, 8, 16384], P(None, 'tm', 'src')
- solution_source: float32 [5, 524288], P(None, ('src', 'tm'))
- solution_knot: float32 [3, 8, 16384], P(None, 'tm', 'src')
- recurrence_next: float32 [4], replicated
Inputs may be any that keep to these rules, and one draw needn't show every extreme that they name: `bucket_fill`: in every draw one bucket of some group block holds exactly 256 observations. Call band_start // 64 the knot owner of a slot. Among the 8 x 256 slots of one column block of 256, each knot owner is named at most 64 times, and in every block some owner exactly 64 times.
All inputs are finite; a program needn't handle non-finite values.
Results may differ from a plain program's by a relative error of at most 0.00002.
Values sent between devices are 32-bit elements; how exact they have to be, the bound alone decides.
A program may use at most 64 MiB of HBM per device.

v0:
```python
import jax
import jax.numpy as jnp
from jax import lax
from jax.sharding import PartitionSpec as P

KB = 4


EPSILON = 1e-06


def band_positions(band_start, knots_slab):
    rows = jnp.arange(3 * KB, dtype=jnp.int32)
    base = rows // KB * knots_slab + rows % KB
    return base[:, None, None] + KB * band_start[None]


def shards(
    left_vector,
    source_coeffs,
    knot_coeffs,
    source_index,
    band_start,
    bucket_fill,
    source_vector,
    knot_vector,
    source_search,
    knot_search,
    source_solution,
    knot_solution,
    recurrence,
):
    slab_count = lax.axis_size("tm")
    group_count = lax.axis_size("src")
    devices = slab_count * group_count
    buckets, capacity = left_vector.shape
    source_dev = source_vector.shape[1]
    knot_dev = knot_vector.shape[2]
    knots_slab = knot_dev * group_count
    total_obs = buckets * capacity * devices
    unknowns = (5 * source_dev + 3 * knot_dev) * devices
    ratio = unknowns / total_obs
    alpha = recurrence[0]
    pivot = recurrence[1]
    remainder = recurrence[2]
    slot = lax.broadcasted_iota(jnp.int32, (buckets, capacity), 1)
    valid = (slot < bucket_fill).astype(jnp.float32)
    flat_source = source_index.reshape(-1)
    picked = jnp.take(source_vector, flat_source, axis=1).reshape(5, buckets, capacity)
    image = jnp.sum(source_coeffs * picked, axis=0)
    own_knots = knot_vector[:, 0, :]
    slab_whole = lax.all_gather(own_knots, "src", axis=1, tiled=True).reshape(-1)
    positions = band_positions(band_start, knots_slab)
    knot_image = jnp.sum(knot_coeffs * jnp.take(slab_whole, positions), axis=0)
    returned = lax.all_to_all(knot_image, "tm", split_axis=0, concat_axis=0, tiled=True)
    raw = valid * (image + returned - alpha * left_vector)
    own_squares = jnp.sum(raw * raw)
    beta = jnp.sqrt(lax.psum(own_squares, ("src", "tm")) / total_obs + EPSILON)
    outgoing = raw / beta
    arrived = lax.all_to_all(outgoing, "tm", split_axis=0, concat_axis=0, tiled=True)
    gradient_source = (
        jnp.zeros((5, source_dev), jnp.float32)
        .at[:, flat_source]
        .add((source_coeffs * outgoing[None]).reshape(5, -1))
    )
    knot_terms = (
        jnp.zeros((3 * knots_slab,), jnp.float32)
        .at[positions.reshape(-1)]
        .add((knot_coeffs * arrived[None]).reshape(-1))
        .reshape(3, knots_slab)
    )
    knot_totals = lax.psum(knot_terms, "src")
    gradient_knot = lax.dynamic_slice_in_dim(
        knot_totals, lax.axis_index("src") * knot_dev, knot_dev, 1
    )
    source_raw = ratio * gradient_source - beta * source_vector
    knot_raw = ratio * gradient_knot - beta * own_knots
    squares = jnp.sum(source_raw * source_raw) + jnp.sum(knot_raw * knot_raw)
    alpha_next = jnp.sqrt(lax.psum(squares, ("src", "tm")) / unknowns + EPSILON)
    left_next = raw / beta
    source_next = source_raw / alpha_next
    knot_next = knot_raw / alpha_next
    radius = jnp.sqrt(pivot * pivot + beta * beta)
    cosine = pivot / radius
    sine = beta / radius
    coupling = sine * alpha_next
    step_gain = cosine * remainder
    solution_source = source_solution + step_gain / radius * source_search
    solution_knot = knot_solution + step_gain / radius * knot_search
    search_source = source_next - coupling / radius * source_search
    search_knot = knot_next[:, None, :] - coupling / radius * knot_search
    recurrence_next = jnp.stack([alpha_next, beta, -cosine * alpha_next, sine * remainder])
    return (
        left_next,
        source_next,
        knot_next[:, None, :],
        search_source,
        search_knot,
        solution_source,
        solution_knot,
        recurrence_next,
    )


def solution(mesh):
    in_specs = (
        P(None, ("src", "tm")),
        P(None, None, ("src", "tm")),
        P(None, None, ("src", "tm")),
        P(None, ("src", "tm")),
        P(None, ("src", "tm")),
        P(None, ("src", "tm")),
        P(None, ("src", "tm")),
        P(None, "tm", "src"),
        P(None, ("src", "tm")),
        P(None, "tm", "src"),
        P(None, ("src", "tm")),
        P(None, "tm", "src"),
        P(),
    )
    out_specs = (
        P(None, ("src", "tm")),
        P(None, ("src", "tm")),
        P(None, "tm", "src"),
        P(None, ("src", "tm")),
        P(None, "tm", "src"),
        P(None, ("src", "tm")),
        P(None, "tm", "src"),
        P(),
    )
    return jax.shard_map(shards, mesh=mesh, in_specs=in_specs, out_specs=out_specs, check_vma=False)
```

profile of v0, /device:TPU:1, one launch (start us, length us, event | category | flops | bytes accessed | tf_op | source)
XLA Modules:
  0.0 866.1 jit_solution(7644518561160794615)
XLA Ops:
  7.2 0.0 copy-start.8
  7.2 71.3 %all-gather = f32[3,1,16384]{2,1,0:T(1,128)S(1)} all-gather(f32[3,1,256]{2,1,0:T(1,128)} %param.20), channel_id=2, replica_groups=mesh['src'=64,'tm'=8] {'src'}, dimensions={2}, use_global_device_ids=true | all-gather | bytes 199680 | tf_op jit(solution)/shard_map/all_gather | solution.py:52
  78.5 0.1 fusion.2
  78.6 0.1 copy.62
  78.7 135.5 %gather_fusion.1 = f32[24576]{0:T(1024)S(1)} fusion(f32[49152]{0:T(1024)S(1)} %bitcast.46, s32[24576]{0:T(1024)S(1)} %broadcast_clamp_fusion), kind=kCustom, calls=%fused_computation.1 | custom fusion | bytes 294912 | tf_op jit(solution)/shard_map/jit(_take)/gather | solution.py:54
  214.2 0.0 copy-start
  214.3 0.8 copy-done
  215.1 0.1 multiply_reduce_fusion
  215.2 0.6 all_to_all.14
  215.8 23.8 %all-to-all-start = ((f32[8,1,256]{2,1,0:T(1,128)}), f32[8,1,256]{2,1,0:T(1,128)S(1)}, u32[]{:S(2)}, u32[]{:S(2)}) async-start(f32[8,1,256]{2,1,0:T(1,128)} %all_to_all.14), calls=%async_computation | async-start | bytes 16384 | tf_op jit(solution)/shard_map/all_to_all | solution.py:55
  239.7 0.1 broadcast_add_fusion
  239.7 0.7 copy-done.1
  240.4 0.2 copy.52
  240.6 0.5 copy-done.5
  241.2 5.5 gather_fusion
  246.7 0.0 copy-start.10
  246.7 0.3 copy.53
  247.0 0.1 add.175
  247.1 0.0 copy-start.2
  247.1 0.1 compare_select_fusion
  247.2 0.7 copy-done.2
  247.9 0.6 fusion.10
  249.8 0.0 copy-start.13
  249.8 0.7 copy-done.9
  250.5 1.3 multiply_reduce_fusion.3
  251.8 101.1 %psum.21 = f32[]{:T(128)} all-reduce(f32[]{:T(128)} %get-tuple-element.34), channel_id=1, replica_groups=mesh['src'=64,'tm'=8] {'src','tm'}, use_global_device_ids=true, to_apply=%region_3.4 | all-reduce | flops 1 | bytes 8 | tf_op jit(solution)/shard_map/psum | solution.py:58
  353.6 0.6 copy.56
  354.2 3.9 all-to-all-start.1
  358.2 4.6 all-to-all-done.1
  362.8 0.1 copy.63
  362.9 128.4 %scatter_custom_fusion.1 = f32[49152]{0:T(1024)S(1)} fusion(s32[24576]{0:T(1024)S(1)} %bitcast.50, f32[24576]{0:T(1024)S(1)} %bitcast.51, f32[]{:T(128)} %constant.77.clone.1), kind=kCustom, calls=%fused_computation.11 | custom fusion | flops 24576 | bytes 196612 | tf_op jit(solution)/shard_map/scatter-add | solution.py:69
  491.3 0.8 reshape.152
  492.1 0.0 all-reduce.2.cloned.1.call-update
  492.9 0.4 copy.58
  493.3 11.6 %scatter_custom_fusion = f32[5,1024]{0,1:T(8,128)S(1)} fusion(s32[2048]{0:T(1024)S(1)} %bitcast.55, f32[2048,5]{1,0:T(8,128)S(1)} %bitcast.48, f32[]{:T(128)} %constant.77.clone.1), kind=kCustom, calls=%fused_computation.7 | custom fusion | flops 10240 | bytes 20484 | tf_op jit(solution)/shard_map/scatter-add | solution.py:64
  504.9 0.2 copy.55
  505.8 0.0 copy-start.7
  505.8 0.6 multiply_reduce_fusion.2
  506.4 236.0 %all-reduce.2.cloned.1.call-done = f32[3,16384]{1,0:T(4,128)} async-done(((f32[3,16384]{1,0:T(4,128)}), f32[3,16384]{1,0:T(4,128)}) %all-reduce.2.cloned.1.call-update) | async-done | bytes 196624 | tf_op jit(solution)/shard_map/psum | solution.py:72
  742.4 1.3 multiply_reduce_fusion.4
  745.7 109.7 %psum.23 = f32[]{:T(128)} all-reduce(f32[]{:T(128)S(6)} %add.179), channel_id=1, replica_groups=mesh['src'=64,'tm'=8] {'src','tm'}, use_global_device_ids=true, to_apply=%region_9.10 | all-reduce | flops 1 | bytes 8 | tf_op jit(solution)/shard_map/psum | solution.py:79
  856.1 0.7 broadcast_divide_fusion.2
  856.8 0.6 broadcast_in_dim.37
  857.4 0.7 multiply_subtract_fusion
  858.1 0.0 copy-done.11
  858.1 0.0 copy-done.12
  858.1 0.6 multiply_add_fusion.1
  858.7 0.6 pad_maximum_fusion
  (31 shorter events, 0.2 us)
Async XLA Ops:
  7.2 71.3 %copy-start.8 = (s32[8,256]{1,0:T(8,128)S(1)}, s32[8,256]{1,0:T(8,128)}, u32[]{:S(2)}) copy-start(s32[8,256]{1,0:T(8,128)} %param.17) | copy-start | bytes 24580
  214.2 0.9 copy-start
  215.8 34.0 %all-to-all-start = ((f32[8,1,256]{2,1,0:T(1,128)}), f32[8,1,256]{2,1,0:T(1,128)S(1)}, u32[]{:S(2)}, u32[]{:S(2)}) async-start(f32[8,1,256]{2,1,0:T(1,128)} %all_to_all.14), calls=%async_computation | async-start | bytes 16384 | tf_op jit(solution)/shard_map/all_to_all | solution.py:55
  239.7 0.8 copy-start.1
  240.4 0.7 copy-start.5
  246.7 1.3 copy-start.10
  247.1 0.8 copy-start.2
  249.8 0.7 copy-start.9
  249.8 0.7 copy-start.13
  354.2 8.6 all-to-all-start.1
  358.2 384.2 %all-reduce.2.cloned.1.call-start = ((), (), s32[]{:S(2)}) async-start(), calls=%async_computation.2 | async-start | bytes 524288 | tf_op jit(solution)/shard_map/psum | solution.py:72
  358.2 134.0 %copy-start.6 = (f32[8,256]{1,0:T(8,128)}, f32[8,256]{1,0:T(8,128)S(1)}, u32[]{:S(2)}) copy-start(f32[8,256]{1,0:T(8,128)S(1)} %broadcast_divide_fusion.1) | copy-start | bytes 24580
  505.8 236.6 %copy-start.7 = (f32[3,1,256]{2,1,0:T(1,128)S(1)}, f32[3,1,256]{2,1,0:T(1,128)}, u32[]{:S(2)}) copy-start(f32[3,1,256]{2,1,0:T(1,128)} %param.20) | copy-start | bytes 9220
  505.8 351.6 %copy-start.4 = (f32[5,1024]{1,0:T(8,128)S(1)}, f32[5,1024]{1,0:T(8,128)}, u32[]{:S(2)}) copy-start(f32[5,1024]{1,0:T(8,128)} %param.23) | copy-start | bytes 61444
  506.4 351.0 %copy-start.3 = (f32[5,1024]{1,0:T(8,128)S(1)}, f32[5,1024]{1,0:T(8,128)}, u32[]{:S(2)}) copy-start(f32[5,1024]{1,0:T(8,128)} %param.21) | copy-start | bytes 61444
  857.4 0.7 copy-start.11
  857.4 0.7 copy-start.12
Sparse Core Ops, SparseCore 0:
  492.3 250.1 all-reduce.1
where the time goes:
time: 867 us; the launch traced here: 866 us
  blocking collectives  282 us (33%)
  waiting for transfers between devices  241 us (28%)
  local copies, waits for them, and re-layouts  149 us (17%)
  other arithmetic  146 us (17%)
  starting transfers between devices  27.8 us (3%)
  between operations  20.4 us (2%)
    psum x1, waiting for transfers between devices, shards(): knot_totals = lax.psum(knot_terms, 'src')  236 us
    gather x2, local copies, waits for them, and re-layouts, shards(): knot_image = jnp.sum(knot_coeffs * jnp.take(slab_whole, positions), axis=0)  136 us
    scatter-add x1, other arithmetic, shards(): knot_terms = jnp.zeros((3 * knots_slab,), jnp.float32).at[positions.resha...  128 us
    psum x1, blocking collectives, shards(): alpha_next = jnp.sqrt(lax.psum(squares, ('src', 'tm')) / unknowns + EPSILON)  110 us
    psum x1, blocking collectives, shards(): beta = jnp.sqrt(lax.psum(own_squares, ('src', 'tm')) / total_obs + EPSILON)  101 us
    all_gather x1, blocking collectives, shards(): lax.all_gather(own_knots, 'src', axis=1, tiled=True).reshape(-1)  71.3 us
    all_to_all x1, starting transfers between devices, shards(): lax.all_to_all(knot_image, 'tm', split_axis=0, concat_axis=0, tiled=True)  23.8 us
  transfers between devices with their start and end apart: 3, of which 2 were waited for; matrix products, arithmetic and copies ran while one was open for 2% of the time, Pallas kernels for 0%

commit v1 on v0

v1 whole, which is shorter than its diff:
```python
import functools

import jax
import jax.numpy as jnp
from jax import lax
from jax.experimental import pallas as pl
from jax.experimental.pallas import tpu as pltpu
from jax.sharding import PartitionSpec as P

KB = 4
EPSILON = 1e-06
F32 = jnp.float32
BF16 = jnp.bfloat16
NT = (((1,), (1,)), ((), ()))
NN = (((1,), (0,)), ((), ()))


def split3(x):
    hi = x.astype(BF16)
    rest = x - hi.astype(F32)
    mid = rest.astype(BF16)
    low = (rest - mid.astype(F32)).astype(BF16)
    return hi, mid, low


def split3_f32(x):
    return [part.astype(F32) for part in split3(x)]


def iterate(
    n_src,
    n_tm,
    total_obs,
    unknowns,
    left_ref,
    sc_ref,
    kc_ref,
    si_ref,
    bs_ref,
    fill_ref,
    sv_ref,
    kv_ref,
    rec_ref,
    raw_out,
    sraw_out,
    kraw_out,
    scal_out,
    ag,
    pbuf,
    prcv,
    rbuf,
    rrcv,
    rs_send,
    rs_recv,
    ar1a,
    ar1b,
    ar2a,
    ar2b,
    ohs,
    ohk,
    acc,
    tsend,
    ssem,
    agr,
    prr,
    rrr,
    rsr,
    ar1ar,
    ar1br,
    ar2ar,
    ar2br,
    agss,
    prs,
    rrs,
    rss,
    ar1as,
    ar1bs,
    ar2as,
    ar2bs,
):
    s = lax.axis_index("src")
    m = lax.axis_index("tm")
    ratio = unknowns / total_obs
    cap = left_ref.shape[1]

    def each(n, f):
        lax.fori_loop(1, n, lambda d, c: (f(d), c)[1], 0)

    def src_copy(d, src, dst, send, recv):
        o = lax.rem(s + d, n_src)
        return pltpu.make_async_remote_copy(
            src_ref=src(o),
            dst_ref=dst,
            send_sem=send.at[d],
            recv_sem=recv.at[s],
            device_id={"src": o},
            device_id_type=pl.DeviceIdType.MESH,
        )

    def src_arrival(d, dst, send, recv):
        o = lax.rem(s + d, n_src)
        return pltpu.make_async_remote_copy(
            src_ref=dst(o),
            dst_ref=dst(o),
            send_sem=send.at[d],
            recv_sem=recv.at[o],
            device_id={"src": o},
            device_id_type=pl.DeviceIdType.MESH,
        )

    def tm_copy(d, src, dst, send, recv):
        o = lax.rem(m + d, n_tm)
        return pltpu.make_async_remote_copy(
            src_ref=src(o),
            dst_ref=dst,
            send_sem=send.at[d],
            recv_sem=recv.at[m],
            device_id={"tm": o},
            device_id_type=pl.DeviceIdType.MESH,
        )

    def tm_arrival(d, dst, send, recv):
        o = lax.rem(m + d, n_tm)
        return pltpu.make_async_remote_copy(
            src_ref=dst(o),
            dst_ref=dst(o),
            send_sem=send.at[d],
            recv_sem=recv.at[o],
            device_id={"tm": o},
            device_id_type=pl.DeviceIdType.MESH,
        )

    barrier = pltpu.get_barrier_semaphore()

    def greet_src(d):
        pl.semaphore_signal(
            barrier, inc=1, device_id={"src": lax.rem(s + d, n_src)}, device_id_type=pl.DeviceIdType.MESH
        )

    def greet_tm(d):
        pl.semaphore_signal(
            barrier, inc=1, device_id={"tm": lax.rem(m + d, n_tm)}, device_id_type=pl.DeviceIdType.MESH
        )

    each(n_src, greet_src)
    each(n_tm, greet_tm)

    for a in range(3):
        for sub in range(2):
            ag[s, a * 2 + sub : a * 2 + sub + 1, :] = kv_ref[a, :, sub * 128 : (sub + 1) * 128]

    alpha = rec_ref[0]
    pad3 = jnp.zeros((3, 128), F32)
    table = jnp.concatenate(
        [jnp.concatenate([sv_ref[:, l * 128 : (l + 1) * 128], pad3], axis=0) for l in range(8)], axis=0
    )
    stable = jnp.concatenate(split3(table), axis=1)
    rows128 = lax.broadcasted_iota(jnp.int32, (128, cap), 0)
    lane = lax.broadcasted_iota(jnp.int32, (1, cap), 1)

    for t in range(n_tm):
        idx = si_ref[t : t + 1, :]
        hi = jnp.bitwise_and(idx, 127)
        lo = jnp.right_shift(idx, 7)
        oh = jnp.where(rows128 == hi, 1.0, 0.0).astype(BF16)
        ohs[t] = oh
        found = lax.dot_general(
            stable, jnp.concatenate([oh, oh, oh], axis=0), NN, preferred_element_type=F32
        )
        picked = jnp.zeros((8, cap), F32)
        for l in range(8):
            picked = picked + jnp.where(lo == l, found[l * 8 : (l + 1) * 8], 0.0)
        coef = sc_ref[:, t, :]
        image = jnp.sum(coef * picked[0:5], axis=0, keepdims=True)
        pbuf[t, 0:1, :] = image - alpha * left_ref[t : t + 1, :]
        pbuf[t, 1:2, :] = jnp.where(lane < fill_ref[t : t + 1, :], 1.0, 0.0)

    pl.semaphore_wait(barrier, n_src + n_tm - 2)

    each(n_src, lambda d: src_copy(d, lambda o: ag.at[s, pl.ds(0, 6)], ag.at[s, pl.ds(0, 6)], agss, agr).start())
    each(n_tm, lambda d: tm_copy(d, lambda o: pbuf.at[o], prcv.at[m], prs, prr).start())
    prcv[m] = pbuf[m]

    for i in range(n_tm):
        band = bs_ref[i : i + 1, :]
        hi = jnp.bitwise_and(jnp.right_shift(band, 5), 1) * 64 + jnp.right_shift(band, 6)
        ohk[i] = jnp.where(rows128 == hi, 1.0, 0.0).astype(BF16)

    each(n_tm, lambda d: tm_arrival(d, lambda o: prcv.at[o], prs, prr).wait_recv())
    each(n_src, lambda d: src_arrival(d, lambda o: ag.at[o, pl.ds(0, 6)], agss, agr).wait_recv())

    parts = []
    for a in range(3):
        whole = jnp.concatenate([ag[:, a * 2 + sub, :] for sub in range(2)], axis=0)
        parts.append(jnp.concatenate(split3(jnp.transpose(whole)), axis=1))
    ktable = jnp.concatenate(parts, axis=0)

    band_rows = jnp.right_shift(rows128, 2)
    total = jnp.zeros((1, cap), F32)
    acc[...] = jnp.zeros_like(acc)
    for i in range(n_tm):
        oh = ohk[i]
        found = lax.dot_general(
            ktable, jnp.concatenate([oh, oh, oh], axis=0), NN, preferred_element_type=F32
        )
        lo = jnp.bitwise_and(bs_ref[i : i + 1, :], 31)
        hit = band_rows == lo
        coefs = []
        mixed = None
        for a in range(3):
            four = kc_ref[a * 4 : a * 4 + 4, i, :]
            eight = jnp.concatenate([four, four], axis=0)
            coefs.append(eight)
            term = found[a * 128 : (a + 1) * 128].reshape(16, 8, cap) * eight[None]
            mixed = term if mixed is None else mixed + term
        image = jnp.sum(jnp.where(hit, mixed.reshape(128, cap), 0.0), axis=0, keepdims=True)
        raw = prcv[i, 1:2, :] * (prcv[i, 0:1, :] + image)
        rbuf[i] = raw
        total = total + raw * raw
        hit_b = jnp.where(hit, 1.0, 0.0).astype(BF16)
        spread = [[], [], []]
        for a in range(3):
            for q, part in enumerate(split3_f32(coefs[a] * raw)):
                two = jnp.concatenate([part, part], axis=0).astype(BF16)
                spread[q].append(hit_b * jnp.concatenate([two] * 8, axis=0))
        terms = jnp.concatenate([jnp.concatenate(rows, axis=0) for rows in spread], axis=1)
        acc[...] += lax.dot_general(
            terms, jnp.concatenate([oh, oh, oh], axis=1), NT, preferred_element_type=F32
        )

    ar1a[s] = jnp.broadcast_to(jnp.sum(total, axis=1, keepdims=True), (1, 128))
    for a in range(3):
        turned = jnp.transpose(acc[a * 128 : (a + 1) * 128, :])
        for sub in range(2):
            rs_send[:, a * 2 + sub, :] = turned[sub * 64 : (sub + 1) * 64]

    each(n_tm, lambda d: tm_copy(d, lambda o: rbuf.at[o], rrcv.at[m], rrs, rrr).start())
    rrcv[m] = rbuf[m]
    each(n_src, lambda d: src_copy(d, lambda o: ar1a.at[s], ar1a.at[s], ar1as, ar1ar).start())
    each(n_src, lambda d: src_copy(d, lambda o: rs_send.at[o, pl.ds(0, 6)], rs_recv.at[s, pl.ds(0, 6)], rss, rsr).start())
    rs_recv[s] = rs_send[s]

    each(n_tm, lambda d: tm_arrival(d, lambda o: rrcv.at[o], rrs, rrr).wait_recv())
    grad = jnp.zeros((64, 128), F32)
    for t in range(n_tm):
        raw = rrcv[t]
        raw_out[t : t + 1, :] = raw
        lo = jnp.right_shift(si_ref[t : t + 1, :], 7)
        coef = jnp.concatenate([sc_ref[:, t, :], jnp.zeros((3, cap), F32)], axis=0)
        spread = []
        for part in split3_f32(coef * raw):
            spread.append(
                jnp.concatenate([jnp.where(lo == l, part, 0.0) for l in range(8)], axis=0).astype(BF16)
            )
        oh = ohs[t]
        grad = grad + lax.dot_general(
            jnp.concatenate(spread, axis=1),
            jnp.concatenate([oh, oh, oh], axis=1),
            NT,
            preferred_element_type=F32,
        )

    each(n_src, lambda d: src_arrival(d, lambda o: ar1a.at[o], ar1as, ar1ar).wait_recv())
    ar1b[m] = jnp.sum(ar1a[...], axis=0)
    each(n_tm, lambda d: tm_copy(d, lambda o: ar1b.at[m], ar1b.at[m], ar1bs, ar1br).start())
    each(n_tm, lambda d: tm_arrival(d, lambda o: ar1b.at[o], ar1bs, ar1br).wait_recv())
    beta = jnp.sqrt(jnp.sum(ar1b[...], axis=0) / total_obs + EPSILON)
    scale = ratio / beta
    squares = jnp.zeros((1, 128), F32)
    for l in range(8):
        own = scale * grad[l * 8 : l * 8 + 5] - beta * sv_ref[:, l * 128 : (l + 1) * 128]
        sraw_out[:, l * 128 : (l + 1) * 128] = own
        squares = squares + jnp.sum(own * own, axis=0, keepdims=True)

    each(n_src, lambda d: src_arrival(d, lambda o: rs_recv.at[o, pl.ds(0, 6)], rss, rsr).wait_recv())
    gathered = jnp.sum(rs_recv[...], axis=0)
    for a in range(3):
        for sub in range(2):
            row = a * 2 + sub
            own = scale * gathered[row : row + 1] - beta * kv_ref[a, :, sub * 128 : (sub + 1) * 128]
            kraw_out[a, :, sub * 128 : (sub + 1) * 128] = own
            squares = squares + own * own

    ar2a[s] = jnp.broadcast_to(jnp.sum(squares, axis=1, keepdims=True), (1, 128))
    each(n_src, lambda d: src_copy(d, lambda o: ar2a.at[s], ar2a.at[s], ar2as, ar2ar).start())
    each(n_src, lambda d: src_arrival(d, lambda o: ar2a.at[o], ar2as, ar2ar).wait_recv())
    ar2b[m] = jnp.sum(ar2a[...], axis=0)
    each(n_tm, lambda d: tm_copy(d, lambda o: ar2b.at[m], ar2b.at[m], ar2bs, ar2br).start())
    each(n_tm, lambda d: tm_arrival(d, lambda o: ar2b.at[o], ar2bs, ar2br).wait_recv())
    alpha_next = jnp.sqrt(jnp.sum(ar2b[...], axis=0) / unknowns + EPSILON)
    scal_out[0:1, :] = alpha_next
    scal_out[1:2, :] = beta

    each(n_src, lambda d: src_copy(d, lambda o: ag.at[s, pl.ds(0, 6)], ag.at[s, pl.ds(0, 6)], agss, agr).wait_send())
    each(n_tm, lambda d: tm_copy(d, lambda o: pbuf.at[o], prcv.at[m], prs, prr).wait_send())
    each(n_tm, lambda d: tm_copy(d, lambda o: rbuf.at[o], rrcv.at[m], rrs, rrr).wait_send())
    each(n_src, lambda d: src_copy(d, lambda o: ar1a.at[s], ar1a.at[s], ar1as, ar1ar).wait_send())
    each(n_src, lambda d: src_copy(d, lambda o: rs_send.at[o, pl.ds(0, 6)], rs_recv.at[s, pl.ds(0, 6)], rss, rsr).wait_send())
    each(n_tm, lambda d: tm_copy(d, lambda o: ar1b.at[m], ar1b.at[m], ar1bs, ar1br).wait_send())
    each(n_src, lambda d: src_copy(d, lambda o: ar2a.at[s], ar2a.at[s], ar2as, ar2ar).wait_send())
    each(n_tm, lambda d: tm_copy(d, lambda o: ar2b.at[m], ar2b.at[m], ar2bs, ar2br).wait_send())


def finish(
    raw_ref,
    sraw_ref,
    kraw_ref,
    scal_ref,
    ss_ref,
    ks_ref,
    sx_ref,
    kx_ref,
    rec_ref,
    left_out,
    snext_out,
    knext_out,
    ssearch_out,
    ksearch_out,
    sx_out,
    kx_out,
    rec_out,
):
    alpha_next = scal_ref[0:1, 0:1]
    beta = scal_ref[1:2, 0:1]
    pivot = rec_ref[1]
    remainder = rec_ref[2]
    radius = jnp.sqrt(pivot * pivot + beta * beta)
    cosine = pivot / radius
    sine = beta / radius
    coupling = sine * alpha_next
    gain = cosine * remainder / radius
    share = coupling / radius
    left_out[...] = raw_ref[...] / beta
    snext = sraw_ref[...] / alpha_next
    snext_out[...] = snext
    ssearch_out[...] = snext - share * ss_ref[...]
    sx_out[...] = sx_ref[...] + gain * ss_ref[...]
    for a in range(3):
        knext = kraw_ref[a] / alpha_next
        knext_out[a] = knext
        ksearch_out[a] = knext - share * ks_ref[a]
        kx_out[a] = kx_ref[a] + gain * ks_ref[a]
    lane = lax.broadcasted_iota(jnp.int32, (1, 4), 1)
    rec_out[...] = jnp.where(
        lane == 0,
        alpha_next,
        jnp.where(lane == 1, beta, jnp.where(lane == 2, -cosine * alpha_next, sine * remainder)),
    )


def shards(
    left_vector,
    source_coeffs,
    knot_coeffs,
    source_index,
    band_start,
    bucket_fill,
    source_vector,
    knot_vector,
    source_search,
    knot_search,
    source_solution,
    knot_solution,
    recurrence,
):
    n_tm = lax.axis_size("tm")
    n_src = lax.axis_size("src")
    devices = n_tm * n_src
    buckets, cap = left_vector.shape
    source_dev = source_vector.shape[1]
    knot_dev = knot_vector.shape[2]
    total_obs = buckets * cap * devices
    unknowns = (5 * source_dev + 3 * knot_dev) * devices
    vmem = pl.BlockSpec(memory_space=pltpu.VMEM)
    smem = pl.BlockSpec(memory_space=pltpu.SMEM)
    sem = pltpu.SemaphoreType.DMA
    sem_sizes = [n_src, n_tm, n_tm, n_src, n_src, n_tm, n_src, n_tm]
    raw, sraw, kraw, scal = pl.pallas_call(
        functools.partial(iterate, n_src, n_tm, total_obs, unknowns),
        out_shape=(
            jax.ShapeDtypeStruct((buckets, cap), F32),
            jax.ShapeDtypeStruct((5, source_dev), F32),
            jax.ShapeDtypeStruct((3, 1, knot_dev), F32),
            jax.ShapeDtypeStruct((2, 128), F32),
        ),
        in_specs=[vmem] * 8 + [smem],
        out_specs=[vmem] * 4,
        scratch_shapes=[
            pltpu.VMEM((n_src, 8, 128), F32),
            pltpu.VMEM((n_tm, 2, cap), F32),
            pltpu.VMEM((n_tm, 2, cap), F32),
            pltpu.VMEM((n_tm, 1, cap), F32),
            pltpu.VMEM((n_tm, 1, cap), F32),
            pltpu.VMEM((n_src, 8, 128), F32),
            pltpu.VMEM((n_src, 8, 128), F32),
            pltpu.VMEM((n_src, 1, 128), F32),
            pltpu.VMEM((n_tm, 1, 128), F32),
            pltpu.VMEM((n_src, 1, 128), F32),
            pltpu.VMEM((n_tm, 1, 128), F32),
            pltpu.VMEM((n_tm, 128, cap), BF16),
            pltpu.VMEM((n_tm, 128, cap), BF16),
            pltpu.VMEM((384, 128), F32),
            pltpu.VMEM((8, 128), F32),
            pltpu.SemaphoreType.DMA,
        ]
        + [sem((n,)) for n in sem_sizes]
        + [sem((n,)) for n in sem_sizes],
        compiler_params=pltpu.CompilerParams(collective_id=0, has_side_effects=True),
    )(
        left_vector,
        source_coeffs,
        knot_coeffs,
        source_index,
        band_start,
        bucket_fill,
        source_vector,
        knot_vector,
        recurrence,
    )
    outs = pl.pallas_call(
        finish,
        out_shape=(
            jax.ShapeDtypeStruct((buckets, cap), F32),
            jax.ShapeDtypeStruct((5, source_dev), F32),
            jax.ShapeDtypeStruct((3, 1, knot_dev), F32),
            jax.ShapeDtypeStruct((5, source_dev), F32),
            jax.ShapeDtypeStruct((3, 1, knot_dev), F32),
            jax.ShapeDtypeStruct((5, source_dev), F32),
            jax.ShapeDtypeStruct((3, 1, knot_dev), F32),
            jax.ShapeDtypeStruct((1, 4), F32),
        ),
        in_specs=[vmem] * 8 + [smem],
        out_specs=[vmem] * 8,
    )(raw, sraw, kraw, scal, source_search, knot_search, source_solution, knot_solution, recurrence)
    return (*outs[:7], outs[7].reshape(4))


def solution(mesh):
    in_specs = (
        P(None, ("src", "tm")),
        P(None, None, ("src", "tm")),
        P(None, None, ("src", "tm")),
        P(None, ("src", "tm")),
        P(None, ("src", "tm")),
        P(None, ("src", "tm")),
        P(None, ("src", "tm")),
        P(None, "tm", "src"),
        P(None, ("src", "tm")),
        P(None, "tm", "src"),
        P(None, ("src", "tm")),
        P(None, "tm", "src"),
        P(),
    )
    out_specs = (
        P(None, ("src", "tm")),
        P(None, ("src", "tm")),
        P(None, "tm", "src"),
        P(None, ("src", "tm")),
        P(None, "tm", "src"),
        P(None, ("src", "tm")),
        P(None, "tm", "src"),
        P(),
    )
    return jax.shard_map(shards, mesh=mesh, in_specs=in_specs, out_specs=out_specs, check_vma=False)
```

time: 867 us -> 74.3 us (0.09)
  blocking collectives: 282 us -> 0 us
  waiting for transfers between devices: 241 us -> 0 us
  local copies, waits for them, and re-layouts: 149 us -> 1.32 us
  other arithmetic: 146 us -> 0 us
  Pallas kernels: 0 us -> 72.1 us
  starting transfers between devices: 27.8 us -> 0 us
  between operations: 20.4 us -> 0.64 us
    psum x1 -> x0, waiting for transfers between devices: 236 us -> none  [shards(): knot_totals = lax.psum(knot_terms, 'src')]
    psum x2 -> x0, blocking collectives: 211 us -> none  [the longest x1 110 us: shards(): alpha_next = jnp.sqrt(lax.psum(squares, ('src', 'tm')) / unknowns + EPSILON)]
    gather x4 -> x0, local copies, waits for them, and re-layouts: 141 us -> none  [the longest x2 136 us: shards(): knot_image = jnp.sum(knot_coeffs * jnp.take(slab_whole, positions), axis=0)]
    scatter-add x2 -> x0, other arithmetic: 140 us -> none  [the longest x1 128 us: shards(): knot_terms = jnp.zeros((3 * knots_slab,), jnp.float32).at[positions.resha...]
    pallas_call x0 -> x2, Pallas kernels: none -> 72.1 us  [the longest x1 70.6 us: shards(): pl.pallas_call(functools.partial(iterate, n_src, n_tm, total_obs, unknown...]
    all_gather x1 -> x0, blocking collectives: 71.3 us -> none  [shards(): lax.all_gather(own_knots, 'src', axis=1, tiled=True).reshape(-1)]
    all_to_all x2 -> x0, starting transfers between devices: 27.8 us -> none  [the longest x1 23.8 us: shards(): lax.all_to_all(knot_image, 'tm', split_axis=0, concat_axis=0, tiled=True)]
  transfers between devices with their start and end apart: 3 -> 0, of which waited for: 2 -> 0; matrix products, arithmetic and copies ran while one was open for 2% -> 0% of each run, Pallas kernels for 0% -> 0%
where the time goes in v1:
time: 74.3 us; the launch traced here: 74.1 us
  Pallas kernels  72.1 us (97%)
  local copies, waits for them, and re-layouts  1.32 us (2%)
    pallas_call x1, Pallas kernels, shards(): pl.pallas_call(functools.partial(iterate, n_src, n_tm, total_obs, unknown...  70.6 us
    pallas_call x1, Pallas kernels, shards(): pl.pallas_call(finish, out_shape=(jax.ShapeDtypeStruct((buckets, cap), F3...  1.55 us

profile of v1, /device:TPU:1, one launch (start us, length us, event | category | flops | bytes accessed | tf_op | source)
XLA Modules:
  0.0 74.1 jit_solution(14827722331822637396)
XLA Ops:
  0.6 1.3 %copy.21.fill_ref = s32[8,1]{1,0:T(8,128)} copy(s32[8,1]{0,1:T(1,128)} %param.18) | data formatting | bytes 64 | tf_op args[5]
  2.0 70.6 %shard_map.188 = (f32[8,256]{1,0:T(8,128)}, f32[5,1024]{1,0:T(8,128)}, f32[3,1,256]{2,1,0:T(1,128)}, f32[2,128]{1,0:T(2,128)}) custom-call(f32[8,256]{1,0:T(8,128)} %left_ref.1, f32[5,8,256]{2,1,0:T(8,128)} %sc_ref.1, f32[12,8,256]{2,1,0:T(8,128)} %kc_ref.1, s32[8,256]{1,0:T(8,128)} %si_ref.1, s32[8,256]{1,0:T(8,128)} %bs_ref.1, s32[8,1]{1,0:T(8,128)} %copy.21.fill_ref, ...), custom_call_target="tpu_custom_call" | custom-call | tf_op jit(solution)/shard_map/pallas_call | solution.py:378
  72.5 1.5 %shard_map.189 = (f32[8,256]{1,0:T(8,128)}, f32[5,1024]{1,0:T(8,128)}, f32[3,1,256]{2,1,0:T(1,128)}, f32[5,1024]{1,0:T(8,128)}, f32[3,1,256]{2,1,0:T(1,128)}, /*...) custom-call(f32[8,256]{1,0:T(8,128)} %get-tuple-element.20.raw_ref, f32[5,1024]{1,0:T(8,128)} %get-tuple-element.21.sraw_ref, ...), custom_call_target="tpu_custom_call" | custom-call | tf_op jit(solution)/shard_map/pallas_call | solution.py:420

commit v2 on v1

--- a/solution.py
+++ b/solution.py
@@ -7,7 +7,7 @@
 from jax.experimental.pallas import tpu as pltpu
 from jax.sharding import PartitionSpec as P
 
-KB = 4
+N_X = 4
 EPSILON = 1e-06
 F32 = jnp.float32
 BF16 = jnp.bfloat16
@@ -32,19 +32,26 @@
     n_tm,
     total_obs,
     unknowns,
+    left_hbm,
+    sc_hbm,
+    kc_hbm,
+    si_hbm,
+    bs_hbm,
+    sv_hbm,
+    kv_hbm,
+    fill_ref,
+    rec_ref,
+    raw_out,
+    sraw_out,
+    kraw_out,
+    scal_out,
     left_ref,
     sc_ref,
     kc_ref,
     si_ref,
     bs_ref,
-    fill_ref,
     sv_ref,
     kv_ref,
-    rec_ref,
-    raw_out,
-    sraw_out,
-    kraw_out,
-    scal_out,
     ag,
     pbuf,
     prcv,
@@ -59,91 +66,94 @@
     ohs,
     ohk,
     acc,
-    tsend,
-    ssem,
-    agr,
-    prr,
-    rrr,
-    rsr,
-    ar1ar,
-    ar1br,
-    ar2ar,
-    ar2br,
-    agss,
-    prs,
-    rrs,
-    rss,
-    ar1as,
-    ar1bs,
-    ar2as,
-    ar2bs,
+    load_sem,
+    ag_sem,
+    p_sem,
+    r_sem,
+    rs_sem,
+    ar1a_sem,
+    ar1b_sem,
+    ar2a_sem,
+    ar2b_sem,
 ):
     s = lax.axis_index("src")
     m = lax.axis_index("tm")
     ratio = unknowns / total_obs
     cap = left_ref.shape[1]
-
-    def each(n, f):
-        lax.fori_loop(1, n, lambda d, c: (f(d), c)[1], 0)
-
-    def src_copy(d, src, dst, send, recv):
-        o = lax.rem(s + d, n_src)
-        return pltpu.make_async_remote_copy(
-            src_ref=src(o),
-            dst_ref=dst,
-            send_sem=send.at[d],
-            recv_sem=recv.at[s],
-            device_id={"src": o},
+    n_z = n_src // N_X
+    z = lax.div(s, N_X)
+    x = lax.rem(s, N_X)
+    pending = []
+
+    src_order = [n_src // 2] + [sign * d for d in range(n_src // 2 - 1, 0, -1) for sign in (1, -1)]
+    tm_order = list(range(1, n_tm))
+
+    def send_all(axis, order, me, n, src, dst, sems):
+        for d in order:
+            o = lax.rem(me + d + n, n)
+            pltpu.make_async_remote_copy(
+                src_ref=src(o),
+                dst_ref=dst,
+                send_sem=sems.at[0],
+                recv_sem=sems.at[1],
+                device_id={axis: o},
+                device_id_type=pl.DeviceIdType.MESH,
+            ).start()
+
+    def arrived(axis, whole, sems, which):
+        copy = pltpu.make_async_remote_copy(
+            src_ref=whole,
+            dst_ref=whole,
+            send_sem=sems.at[0],
+            recv_sem=sems.at[1],
+            device_id={axis: 0},
             device_id_type=pl.DeviceIdType.MESH,
         )
-
-    def src_arrival(d, dst, send, recv):
-        o = lax.rem(s + d, n_src)
-        return pltpu.make_async_remote_copy(
-            src_ref=dst(o),
-            dst_ref=dst(o),
-            send_sem=send.at[d],
-            recv_sem=recv.at[o],
-            device_id={"src": o},
-            device_id_type=pl.DeviceIdType.MESH,
-        )
-
-    def tm_copy(d, src, dst, send, recv):
-        o = lax.rem(m + d, n_tm)
-        return pltpu.make_async_remote_copy(
-            src_ref=src(o),
-            dst_ref=dst,
-            send_sem=send.at[d],
-            recv_sem=recv.at[m],
-            device_id={"tm": o},
-            device_id_type=pl.DeviceIdType.MESH,
-        )
-
-    def tm_arrival(d, dst, send, recv):
-        o = lax.rem(m + d, n_tm)
-        return pltpu.make_async_remote_copy(
-            src_ref=dst(o),
-            dst_ref=dst(o),
-            send_sem=send.at[d],
-            recv_sem=recv.at[o],
-            device_id={"tm": o},
-            device_id_type=pl.DeviceIdType.MESH,
-        )
+        return copy.wait_recv() if which else copy.wait_send()
+
+    def src_send(src, dst, whole, sems):
+        send_all("src", src_order, s, n_src, src, dst, sems)
+        pending.append(lambda: arrived("src", whole, sems, 0))
+
+    def tm_send(src, dst, whole, sems):
+        send_all("tm", tm_order, m, n_tm, src, dst, sems)
+        pending.append(lambda: arrived("tm", whole, sems, 0))
+
+    src_rest = pl.ds(0, n_src - 1)
+    tm_rest = pl.ds(0, n_tm - 1)
+    six = pl.ds(0, 6)
+
+    def at(dz, dx):
+        return lax.rem(z + dz + n_z, n_z) * N_X + lax.rem(x + dx, N_X)
+
+    near = [(dz, dx) for dz in (4, -4, 3, -3, 2, -2, 1, -1, 0) for dx in (2, 1, 3, 0) if dz or dx]
 
     barrier = pltpu.get_barrier_semaphore()
-
-    def greet_src(d):
-        pl.semaphore_signal(
-            barrier, inc=1, device_id={"src": lax.rem(s + d, n_src)}, device_id_type=pl.DeviceIdType.MESH
-        )
-
-    def greet_tm(d):
+    for dz, dx in near:
+        pl.semaphore_signal(barrier, inc=1, device_id={"src": at(dz, dx)}, device_id_type=pl.DeviceIdType.MESH)
+    for d in tm_order:
         pl.semaphore_signal(
             barrier, inc=1, device_id={"tm": lax.rem(m + d, n_tm)}, device_id_type=pl.DeviceIdType.MESH
         )
 
-    each(n_src, greet_src)
-    each(n_tm, greet_tm)
+    loads = [
+        pltpu.make_async_copy(src, dst, load_sem.at[n])
+        for n, (src, dst) in enumerate(
+            (
+                (kv_hbm, kv_ref),
+                (sv_hbm, sv_ref),
+                (si_hbm, si_ref),
+                (sc_hbm, sc_ref),
+                (left_hbm, left_ref),
+                (bs_hbm, bs_ref),
+                (kc_hbm, kc_ref),
+            )
+        )
+    ]
+    for load in loads:
+        load.start()
+    for load in loads[:5]:
+        load.wait()
 
     for a in range(3):
         for sub in range(2):
@@ -173,21 +183,54 @@
         coef = sc_ref[:, t, :]
         image = jnp.sum(coef * picked[0:5], axis=0, keepdims=True)
         pbuf[t, 0:1, :] = image - alpha * left_ref[t : t + 1, :]
-        pbuf[t, 1:2, :] = jnp.where(lane < fill_ref[t : t + 1, :], 1.0, 0.0)
-
-    pl.semaphore_wait(barrier, n_src + n_tm - 2)
-
-    each(n_src, lambda d: src_copy(d, lambda o: ag.at[s, pl.ds(0, 6)], ag.at[s, pl.ds(0, 6)], agss, agr).start())
-    each(n_tm, lambda d: tm_copy(d, lambda o: pbuf.at[o], prcv.at[m], prs, prr).start())
+        pbuf[t, 1:2, :] = jnp.where(lane < fill_ref[t], 1.0, 0.0)
+
+    pl.semaphore_wait(barrier, len(near) + n_tm - 1)
+
+    def hand_on(block, target, which):
+        pltpu.make_async_remote_copy(
+            src_ref=block,
+            dst_ref=block,
+            send_sem=ag_sem.at[0],
+            recv_sem=ag_sem.at[which],
+            device_id={"src": target},
+            device_id_type=pl.DeviceIdType.MESH,
+        ).start()
+
+    def taken(blocks, which):
+        whole = ag.at[pl.ds(0, blocks), six]
+        copy = pltpu.make_async_remote_copy(
+            src_ref=whole,
+            dst_ref=whole,
+            send_sem=ag_sem.at[0],
+            recv_sem=ag_sem.at[which],
+            device_id={"src": s},
+            device_id_type=pl.DeviceIdType.MESH,
+        )
+        return copy.wait_recv() if which else copy.wait_send()
+
+    for dz, dx in near:
+        hand_on(ag.at[s, six], at(dz, dx), 1 if dz == 4 else 2 if dz == -4 else 3)
+    pending.append(lambda: taken(n_src - 1, 0))
+    tm_send(lambda o: pbuf.at[o], prcv.at[m], pbuf.at[tm_rest], p_sem)
     prcv[m] = pbuf[m]
+    for which, sign, reach in ((1, 1, 4), (2, -1, 3)):
+        taken(N_X, which)
+        plane = ag.at[pl.ds(lax.rem(z - sign * 4 + n_z, n_z) * N_X, N_X), six]
+        for k in range(reach, 0, -1):
+            hand_on(plane, at(sign * k, 0), 4)
+
+    for load in loads[5:]:
+        load.wait()
 
     for i in range(n_tm):
         band = bs_ref[i : i + 1, :]
         hi = jnp.bitwise_and(jnp.right_shift(band, 5), 1) * 64 + jnp.right_shift(band, 6)
         ohk[i] = jnp.where(rows128 == hi, 1.0, 0.0).astype(BF16)
 
-    each(n_tm, lambda d: tm_arrival(d, lambda o: prcv.at[o], prs, prr).wait_recv())
-    each(n_src, lambda d: src_arrival(d, lambda o: ag.at[o, pl.ds(0, 6)], agss, agr).wait_recv())
+    arrived("tm", prcv.at[tm_rest], p_sem, 1)
+    taken(len(near) - 2 * N_X, 3)
+    taken(7 * N_X, 4)
 
     parts = []
     for a in range(3):
@@ -229,18 +272,18 @@
         )
 
     ar1a[s] = jnp.broadcast_to(jnp.sum(total, axis=1, keepdims=True), (1, 128))
+    tm_send(lambda o: rbuf.at[o], rrcv.at[m], rbuf.at[tm_rest], r_sem)
+    rrcv[m] = rbuf[m]
+    src_send(lambda o: ar1a.at[s], ar1a.at[s], ar1a.at[src_rest], ar1a_sem)
     for a in range(3):
         turned = jnp.transpose(acc[a * 128 : (a + 1) * 128, :])
         for sub in range(2):
             rs_send[:, a * 2 + sub, :] = turned[sub * 64 : (sub + 1) * 64]
 
-    each(n_tm, lambda d: tm_copy(d, lambda o: rbuf.at[o], rrcv.at[m], rrs, rrr).start())
-    rrcv[m] = rbuf[m]
-    each(n_src, lambda d: src_copy(d, lambda o: ar1a.at[s], ar1a.at[s], ar1as, ar1ar).start())
-    each(n_src, lambda d: src_copy(d, lambda o: rs_send.at[o, pl.ds(0, 6)], rs_recv.at[s, pl.ds(0, 6)], rss, rsr).start())
+    src_send(lambda o: rs_send.at[o, six], rs_recv.at[s, six], rs_send.at[src_rest, six], rs_sem)
     rs_recv[s] = rs_send[s]
 
-    each(n_tm, lambda d: tm_arrival(d, lambda o: rrcv.at[o], rrs, rrr).wait_recv())
+    arrived("tm", rrcv.at[tm_rest], r_sem, 1)
     grad = jnp.zeros((64, 128), F32)
     for t in range(n_tm):
         raw = rrcv[t]
@@ -260,10 +303,10 @@
             preferred_element_type=F32,
         )
 
-    each(n_src, lambda d: src_arrival(d, lambda o: ar1a.at[o], ar1as, ar1ar).wait_recv())
+    arrived("src", ar1a.at[src_rest], ar1a_sem, 1)
     ar1b[m] = jnp.sum(ar1a[...], axis=0)
-    each(n_tm, lambda d: tm_copy(d, lambda o: ar1b.at[m], ar1b.at[m], ar1bs, ar1br).start())
-    each(n_tm, lambda d: tm_arrival(d, lambda o: ar1b.at[o], ar1bs, ar1br).wait_recv())
+    tm_send(lambda o: ar1b.at[m], ar1b.at[m], ar1b.at[tm_rest], ar1b_sem)
+    arrived("tm", ar1b.at[tm_rest], ar1b_sem, 1)
     beta = jnp.sqrt(jnp.sum(ar1b[...], axis=0) / total_obs + EPSILON)
     scale = ratio / beta
     squares = jnp.zeros((1, 128), F32)
@@ -272,7 +315,7 @@
         sraw_out[:, l * 128 : (l + 1) * 128] = own
         squares = squares + jnp.sum(own * own, axis=0, keepdims=True)
 
-    each(n_src, lambda d: src_arrival(d, lambda o: rs_recv.at[o, pl.ds(0, 6)], rss, rsr).wait_recv())
+    arrived("src", rs_recv.at[src_rest, six], rs_sem, 1)
     gathered = jnp.sum(rs_recv[...], axis=0)
     for a in range(3):
         for sub in range(2):
@@ -282,23 +325,17 @@
             squares = squares + own * own
 
     ar2a[s] = jnp.broadcast_to(jnp.sum(squares, axis=1, keepdims=True), (1, 128))
-    each(n_src, lambda d: src_copy(d, lambda o: ar2a.at[s], ar2a.at[s], ar2as, ar2ar).start())
-    each(n_src, lambda d: src_arrival(d, lambda o: ar2a.at[o], ar2as, ar2ar).wait_recv())
+    src_send(lambda o: ar2a.at[s], ar2a.at[s], ar2a.at[src_rest], ar2a_sem)
+    arrived("src", ar2a.at[src_rest], ar2a_sem, 1)
     ar2b[m] = jnp.sum(ar2a[...], axis=0)
-    each(n_tm, lambda d: tm_copy(d, lambda o: ar2b.at[m], ar2b.at[m], ar2bs, ar2br).start())
-    each(n_tm, lambda d: tm_arrival(d, lambda o: ar2b.at[o], ar2bs, ar2br).wait_recv())
+    tm_send(lambda o: ar2b.at[m], ar2b.at[m], ar2b.at[tm_rest], ar2b_sem)
+    arrived("tm", ar2b.at[tm_rest], ar2b_sem, 1)
     alpha_next = jnp.sqrt(jnp.sum(ar2b[...], axis=0) / unknowns + EPSILON)
     scal_out[0:1, :] = alpha_next
     scal_out[1:2, :] = beta
 
-    each(n_src, lambda d: src_copy(d, lambda o: ag.at[s, pl.ds(0, 6)], ag.at[s, pl.ds(0, 6)], agss, agr).wait_send())
-    each(n_tm, lambda d: tm_copy(d, lambda o: pbuf.at[o], prcv.at[m], prs, prr).wait_send())
-    each(n_tm, lambda d: tm_copy(d, lambda o: rbuf.at[o], rrcv.at[m], rrs, rrr).wait_send())
-    each(n_src, lambda d: src_copy(d, lambda o: ar1a.at[s], ar1a.at[s], ar1as, ar1ar).wait_send())
-    each(n_src, lambda d: src_copy(d, lambda o: rs_send.at[o, pl.ds(0, 6)], rs_recv.at[s, pl.ds(0, 6)], rss, rsr).wait_send())
-    each(n_tm, lambda d: tm_copy(d, lambda o: ar1b.at[m], ar1b.at[m], ar1bs, ar1br).wait_send())
-    each(n_src, lambda d: src_copy(d, lambda o: ar2a.at[s], ar2a.at[s], ar2as, ar2ar).wait_send())
-    each(n_tm, lambda d: tm_copy(d, lambda o: ar2b.at[m], ar2b.at[m], ar2bs, ar2br).wait_send())
+    for wait in pending:
+        wait()
 
 
 def finish(
@@ -373,8 +410,7 @@
     unknowns = (5 * source_dev + 3 * knot_dev) * devices
     vmem = pl.BlockSpec(memory_space=pltpu.VMEM)
     smem = pl.BlockSpec(memory_space=pltpu.SMEM)
-    sem = pltpu.SemaphoreType.DMA
-    sem_sizes = [n_src, n_tm, n_tm, n_src, n_src, n_tm, n_src, n_tm]
+    hbm = pl.BlockSpec(memory_space=pl.ANY)
     raw, sraw, kraw, scal = pl.pallas_call(
         functools.partial(iterate, n_src, n_tm, total_obs, unknowns),
         out_shape=(
@@ -383,9 +419,21 @@
             jax.ShapeDtypeStruct((3, 1, knot_dev), F32),
             jax.ShapeDtypeStruct((2, 128), F32),
         ),
-        in_specs=[vmem] * 8 + [smem],
+        in_specs=[hbm] * 7 + [smem] * 2,
         out_specs=[vmem] * 4,
         scratch_shapes=[
+            pltpu.VMEM(a.shape, a.dtype)
+            for a in (
+                left_vector,
+                source_coeffs,
+                knot_coeffs,
+                source_index,
+                band_start,
+                source_vector,
+                knot_vector,
+            )
+        ]
+        + [
             pltpu.VMEM((n_src, 8, 128), F32),
             pltpu.VMEM((n_tm, 2, cap), F32),
             pltpu.VMEM((n_tm, 2, cap), F32),
@@ -400,11 +448,9 @@
             pltpu.VMEM((n_tm, 128, cap), BF16),
             pltpu.VMEM((n_tm, 128, cap), BF16),
             pltpu.VMEM((384, 128), F32),
-            pltpu.VMEM((8, 128), F32),
-            pltpu.SemaphoreType.DMA,
+            pltpu.SemaphoreType.DMA((7,)),
         ]
-        + [sem((n,)) for n in sem_sizes]
-        + [sem((n,)) for n in sem_sizes],
+        + [pltpu.SemaphoreType.DMA((5,))] + [pltpu.SemaphoreType.DMA((2,))] * 7,
         compiler_params=pltpu.CompilerParams(collective_id=0, has_side_effects=True),
     )(
         left_vector,
@@ -412,9 +458,9 @@
         knot_coeffs,
         source_index,
         band_start,
-        bucket_fill,
         source_vector,
         knot_vector,
+        bucket_fill.reshape(buckets),
         recurrence,
     )
     outs = pl.pallas_call(

time: 74.3 us -> 56.7 us (0.76)
  Pallas kernels: 72.1 us -> 55.8 us
  local copies, waits for them, and re-layouts: 1.32 us -> 0 us
    pallas_call x1, Pallas kernels: 70.6 us -> 54.3 us  [shards(): pl.pallas_call(functools.partial(iterate, n_src, n_tm, total_obs, unknown...]
    unnamed x1 -> x0, local copies, waits for them, and re-layouts: 1.32 us -> none
where the time goes in v2:
time: 56.7 us; the launch traced here: 56.5 us
  Pallas kernels  55.8 us (98%)
  between operations  0.64 us (1%)
    pallas_call x1, Pallas kernels, shards(): pl.pallas_call(functools.partial(iterate, n_src, n_tm, total_obs, unknown...  54.3 us
    pallas_call x1, Pallas kernels, shards(): pl.pallas_call(finish, out_shape=(jax.ShapeDtypeStruct((buckets, cap), F3...  1.55 us

profile of v2, /device:TPU:1, one launch (start us, length us, event | category | flops | bytes accessed | tf_op | source)
XLA Modules:
  0.0 56.5 jit_solution(17028817162200593696)
XLA Ops:
  0.6 54.3 %shard_map.188 = (f32[8,256]{1,0:T(8,128)}, f32[5,1024]{1,0:T(8,128)}, f32[3,1,256]{2,1,0:T(1,128)}, f32[2,128]{1,0:T(2,128)}) custom-call(f32[8,256]{1,0:T(8,128)} %left_hbm.1, f32[5,8,256]{2,1,0:T(8,128)} %sc_hbm.1, f32[12,8,256]{2,1,0:T(8,128)} %kc_hbm.1, s32[8,256]{1,0:T(8,128)} %si_hbm.1, s32[8,256]{1,0:T(8,128)} %bs_hbm.1, f32[5,1024]{1,0:T(8,128)} %sv_hbm.1, ...), custom_call_target="tpu_custom_call" | custom-call | tf_op jit(solution)/shard_map/pallas_call | solution.py:414
  54.9 1.5 %shard_map.189 = (f32[8,256]{1,0:T(8,128)}, f32[5,1024]{1,0:T(8,128)}, f32[3,1,256]{2,1,0:T(1,128)}, f32[5,1024]{1,0:T(8,128)}, f32[3,1,256]{2,1,0:T(1,128)}, /*...) custom-call(f32[8,256]{1,0:T(8,128)} %get-tuple-element.20.raw_ref, f32[5,1024]{1,0:T(8,128)} %get-tuple-element.21.sraw_ref, ...), custom_call_target="tpu_custom_call" | custom-call | tf_op jit(solution)/shard_map/pallas_call | solution.py:466

commit v3 on v2

--- a/solution.py
+++ b/solution.py
@@ -39,12 +39,20 @@
     bs_hbm,
     sv_hbm,
     kv_hbm,
-    fill_ref,
-    rec_ref,
+    fill_hbm,
+    rec_hbm,
+    ss_hbm,
+    ks_hbm,
+    sx_hbm,
+    kx_hbm,
     raw_out,
     sraw_out,
     kraw_out,
     scal_out,
+    ss_out,
+    ks_out,
+    sx_out,
+    kx_out,
     left_ref,
     sc_ref,
     kc_ref,
@@ -52,6 +60,8 @@
     bs_ref,
     sv_ref,
     kv_ref,
+    fill_ref,
+    rec_ref,
     ag,
     pbuf,
     prcv,
@@ -65,7 +75,7 @@
     ar2b,
     ohs,
     ohk,
-    acc,
+    cl,
     load_sem,
     ag_sem,
     p_sem,
@@ -128,6 +138,29 @@
 
     near = [(dz, dx) for dz in (4, -4, 3, -3, 2, -2, 1, -1, 0) for dx in (2, 1, 3, 0) if dz or dx]
 
+    loads = [
+        pltpu.make_async_copy(src, dst, load_sem.at[n])
+        for n, (src, dst) in enumerate(
+            (
+                (kv_hbm, kv_ref),
+                (rec_hbm, rec_ref),
+                (fill_hbm, fill_ref),
+                (sv_hbm, sv_ref),
+                (si_hbm, si_ref),
+                (sc_hbm, sc_ref),
+                (left_hbm, left_ref),
+                (bs_hbm, bs_ref),
+                (kc_hbm, kc_ref),
+                (ss_hbm, ss_out),
+                (ks_hbm, ks_out),
+                (sx_hbm, sx_out),
+                (kx_hbm, kx_out),
+            )
+        )
+    ]
+    for load in loads:
+        load.start()
+
     barrier = pltpu.get_barrier_semaphore()
     for dz, dx in near:
         pl.semaphore_signal(barrier, inc=1, device_id={"src": at(dz, dx)}, device_id_type=pl.DeviceIdType.MESH)
@@ -136,23 +169,7 @@
             barrier, inc=1, device_id={"tm": lax.rem(m + d, n_tm)}, device_id_type=pl.DeviceIdType.MESH
         )
 
-    loads = [
-        pltpu.make_async_copy(src, dst, load_sem.at[n])
-        for n, (src, dst) in enumerate(
-            (
-                (kv_hbm, kv_ref),
-                (sv_hbm, sv_ref),
-                (si_hbm, si_ref),
-                (sc_hbm, sc_ref),
-                (left_hbm, left_ref),
-                (bs_hbm, bs_ref),
-                (kc_hbm, kc_ref),
-            )
-        )
-    ]
-    for load in loads:
-        load.start()
-    for load in loads[:5]:
+    for load in loads[:7]:
         load.wait()
 
     for a in range(3):
@@ -220,70 +237,75 @@
         for k in range(reach, 0, -1):
             hand_on(plane, at(sign * k, 0), 4)
 
-    for load in loads[5:]:
+    for load in loads[7:]:
         load.wait()
 
+    rows256 = lax.broadcasted_iota(jnp.int32, (256, cap), 0)
     for i in range(n_tm):
         band = bs_ref[i : i + 1, :]
-        hi = jnp.bitwise_and(jnp.right_shift(band, 5), 1) * 64 + jnp.right_shift(band, 6)
-        ohk[i] = jnp.where(rows128 == hi, 1.0, 0.0).astype(BF16)
+        hi = (
+            jnp.bitwise_and(jnp.right_shift(band, 4), 1) * 128
+            + jnp.bitwise_and(jnp.right_shift(band, 5), 1) * 64
+            + jnp.right_shift(band, 6)
+        )
+        ohk[i] = jnp.where(rows256 == hi, 1.0, 0.0).astype(BF16)
 
     arrived("tm", prcv.at[tm_rest], p_sem, 1)
     taken(len(near) - 2 * N_X, 3)
     taken(7 * N_X, 4)
 
-    parts = []
+    table = []
     for a in range(3):
-        whole = jnp.concatenate([ag[:, a * 2 + sub, :] for sub in range(2)], axis=0)
-        parts.append(jnp.concatenate(split3(jnp.transpose(whole)), axis=1))
-    ktable = jnp.concatenate(parts, axis=0)
-
-    band_rows = jnp.right_shift(rows128, 2)
+        whole = jnp.concatenate([ag[:, a * 2 + half, :] for half in range(2)], axis=0)
+        turned = jnp.transpose(whole)
+        table.append(jnp.concatenate([turned[0:64], turned[64:128]], axis=1))
+    ktable = jnp.concatenate(split3(jnp.concatenate(table, axis=0)), axis=0)
+
+    band_rows = jnp.right_shift(lax.broadcasted_iota(jnp.int32, (64, cap), 0), 2)
     total = jnp.zeros((1, cap), F32)
-    acc[...] = jnp.zeros_like(acc)
     for i in range(n_tm):
-        oh = ohk[i]
-        found = lax.dot_general(
-            ktable, jnp.concatenate([oh, oh, oh], axis=0), NN, preferred_element_type=F32
-        )
-        lo = jnp.bitwise_and(bs_ref[i : i + 1, :], 31)
-        hit = band_rows == lo
+        three = lax.dot_general(ktable, ohk[i], NN, preferred_element_type=F32)
+        found = three[0:192] + three[192:384] + three[384:576]
+        lo = jnp.bitwise_and(bs_ref[i : i + 1, :], 15)
         coefs = []
         mixed = None
         for a in range(3):
             four = kc_ref[a * 4 : a * 4 + 4, i, :]
             eight = jnp.concatenate([four, four], axis=0)
             coefs.append(eight)
-            term = found[a * 128 : (a + 1) * 128].reshape(16, 8, cap) * eight[None]
+            term = found[a * 64 : (a + 1) * 64].reshape(8, 8, cap) * eight[None]
             mixed = term if mixed is None else mixed + term
-        image = jnp.sum(jnp.where(hit, mixed.reshape(128, cap), 0.0), axis=0, keepdims=True)
+        image = jnp.sum(jnp.where(band_rows == lo, mixed.reshape(64, cap), 0.0), axis=0, keepdims=True)
         raw = prcv[i, 1:2, :] * (prcv[i, 0:1, :] + image)
         rbuf[i] = raw
         total = total + raw * raw
-        hit_b = jnp.where(hit, 1.0, 0.0).astype(BF16)
-        spread = [[], [], []]
         for a in range(3):
             for q, part in enumerate(split3_f32(coefs[a] * raw)):
-                two = jnp.concatenate([part, part], axis=0).astype(BF16)
-                spread[q].append(hit_b * jnp.concatenate([two] * 8, axis=0))
-        terms = jnp.concatenate([jnp.concatenate(rows, axis=0) for rows in spread], axis=1)
-        acc[...] += lax.dot_general(
-            terms, jnp.concatenate([oh, oh, oh], axis=1), NT, preferred_element_type=F32
-        )
-
-    ar1a[s] = jnp.broadcast_to(jnp.sum(total, axis=1, keepdims=True), (1, 128))
+                cl[i, q * 3 + a] = jnp.concatenate([part, part], axis=0).astype(BF16)
+    ar1a[s] = total[:, 0:128] + total[:, 128:256]
+    src_send(lambda o: ar1a.at[s], ar1a.at[s], ar1a.at[src_rest], ar1a_sem)
     tm_send(lambda o: rbuf.at[o], rrcv.at[m], rbuf.at[tm_rest], r_sem)
     rrcv[m] = rbuf[m]
-    src_send(lambda o: ar1a.at[s], ar1a.at[s], ar1a.at[src_rest], ar1a_sem)
+
+    acc = jnp.zeros((192, 256), F32)
+    for i in range(n_tm):
+        lo = jnp.bitwise_and(bs_ref[i : i + 1, :], 15)
+        hit = jnp.where(band_rows == lo, 1.0, 0.0).astype(BF16)
+        terms = jnp.concatenate(
+            [hit * jnp.concatenate([cl[i, row]] * 4, axis=0) for row in range(9)], axis=0
+        )
+        three = lax.dot_general(terms, ohk[i], NT, preferred_element_type=F32)
+        acc = acc + (three[0:192] + three[192:384] + three[384:576])
     for a in range(3):
-        turned = jnp.transpose(acc[a * 128 : (a + 1) * 128, :])
-        for sub in range(2):
-            rs_send[:, a * 2 + sub, :] = turned[sub * 64 : (sub + 1) * 64]
+        own = acc[a * 64 : (a + 1) * 64]
+        turned = jnp.transpose(jnp.concatenate([own[:, 0:128], own[:, 128:256]], axis=0))
+        for half in range(2):
+            rs_send[:, a * 2 + half, :] = turned[half * 64 : (half + 1) * 64]
 
     src_send(lambda o: rs_send.at[o, six], rs_recv.at[s, six], rs_send.at[src_rest, six], rs_sem)
     rs_recv[s] = rs_send[s]
-
     arrived("tm", rrcv.at[tm_rest], r_sem, 1)
+
     grad = jnp.zeros((64, 128), F32)
     for t in range(n_tm):
         raw = rrcv[t]
@@ -307,7 +329,7 @@
     ar1b[m] = jnp.sum(ar1a[...], axis=0)
     tm_send(lambda o: ar1b.at[m], ar1b.at[m], ar1b.at[tm_rest], ar1b_sem)
     arrived("tm", ar1b.at[tm_rest], ar1b_sem, 1)
-    beta = jnp.sqrt(jnp.sum(ar1b[...], axis=0) / total_obs + EPSILON)
+    beta = jnp.sqrt(jnp.sum(jnp.sum(ar1b[...], axis=0), axis=1, keepdims=True) / total_obs + EPSILON)
     scale = ratio / beta
     squares = jnp.zeros((1, 128), F32)
     for l in range(8):
@@ -324,16 +346,31 @@
             kraw_out[a, :, sub * 128 : (sub + 1) * 128] = own
             squares = squares + own * own
 
-    ar2a[s] = jnp.broadcast_to(jnp.sum(squares, axis=1, keepdims=True), (1, 128))
+    ar2b[m] = squares
+    tm_send(lambda o: ar2b.at[m], ar2b.at[m], ar2b.at[tm_rest], ar2b_sem)
+    arrived("tm", ar2b.at[tm_rest], ar2b_sem, 1)
+    ar2a[s] = jnp.sum(ar2b[...], axis=0)
     src_send(lambda o: ar2a.at[s], ar2a.at[s], ar2a.at[src_rest], ar2a_sem)
     arrived("src", ar2a.at[src_rest], ar2a_sem, 1)
-    ar2b[m] = jnp.sum(ar2a[...], axis=0)
-    tm_send(lambda o: ar2b.at[m], ar2b.at[m], ar2b.at[tm_rest], ar2b_sem)
-    arrived("tm", ar2b.at[tm_rest], ar2b_sem, 1)
-    alpha_next = jnp.sqrt(jnp.sum(ar2b[...], axis=0) / unknowns + EPSILON)
-    scal_out[0:1, :] = alpha_next
-    scal_out[1:2, :] = beta
-
+    alpha_next = jnp.sqrt(
+        jnp.sum(jnp.sum(ar2a[...], axis=0), axis=1, keepdims=True) / unknowns + EPSILON
+    )
+    pivot = rec_ref[1]
+    remainder = rec_ref[2]
+    radius = jnp.sqrt(pivot * pivot + beta * beta)
+    cosine = pivot / radius
+    sine = beta / radius
+    wide = (1, 128)
+    lane = lax.broadcasted_iota(jnp.int32, wide, 1)
+    scal_out[0:1, :] = jnp.broadcast_to(alpha_next, wide)
+    scal_out[1:2, :] = jnp.broadcast_to(beta, wide)
+    scal_out[2:3, :] = jnp.broadcast_to(cosine * remainder / radius, wide)
+    scal_out[3:4, :] = jnp.broadcast_to(sine * alpha_next / radius, wide)
+    scal_out[4:5, :] = jnp.where(
+        lane == 0,
+        alpha_next,
+        jnp.where(lane == 1, beta, jnp.where(lane == 2, -cosine * alpha_next, sine * remainder)),
+    )
     for wait in pending:
         wait()
 
@@ -347,7 +384,6 @@
     ks_ref,
     sx_ref,
     kx_ref,
-    rec_ref,
     left_out,
     snext_out,
     knext_out,
@@ -359,14 +395,8 @@
 ):
     alpha_next = scal_ref[0:1, 0:1]
     beta = scal_ref[1:2, 0:1]
-    pivot = rec_ref[1]
-    remainder = rec_ref[2]
-    radius = jnp.sqrt(pivot * pivot + beta * beta)
-    cosine = pivot / radius
-    sine = beta / radius
-    coupling = sine * alpha_next
-    gain = cosine * remainder / radius
-    share = coupling / radius
+    gain = scal_ref[2:3, 0:1]
+    share = scal_ref[3:4, 0:1]
     left_out[...] = raw_ref[...] / beta
     snext = sraw_ref[...] / alpha_next
     snext_out[...] = snext
@@ -377,12 +407,7 @@
         knext_out[a] = knext
         ksearch_out[a] = knext - share * ks_ref[a]
         kx_out[a] = kx_ref[a] + gain * ks_ref[a]
-    lane = lax.broadcasted_iota(jnp.int32, (1, 4), 1)
-    rec_out[...] = jnp.where(
-        lane == 0,
-        alpha_next,
-        jnp.where(lane == 1, beta, jnp.where(lane == 2, -cosine * alpha_next, sine * remainder)),
-    )
+    rec_out[...] = scal_ref[4:5, 0:4]
 
 
 def shards(
@@ -409,18 +434,21 @@
     total_obs = buckets * cap * devices
     unknowns = (5 * source_dev + 3 * knot_dev) * devices
     vmem = pl.BlockSpec(memory_space=pltpu.VMEM)
-    smem = pl.BlockSpec(memory_space=pltpu.SMEM)
     hbm = pl.BlockSpec(memory_space=pl.ANY)
-    raw, sraw, kraw, scal = pl.pallas_call(
+    held = pl.pallas_call(
         functools.partial(iterate, n_src, n_tm, total_obs, unknowns),
         out_shape=(
-            jax.ShapeDtypeStruct((buckets, cap), F32),
-            jax.ShapeDtypeStruct((5, source_dev), F32),
-            jax.ShapeDtypeStruct((3, 1, knot_dev), F32),
-            jax.ShapeDtypeStruct((2, 128), F32),
+            pltpu.VMEM((buckets, cap), F32),
+            pltpu.VMEM((5, source_dev), F32),
+            pltpu.VMEM((3, 1, knot_dev), F32),
+            pltpu.VMEM((8, 128), F32),
+            pltpu.VMEM((5, source_dev), F32),
+            pltpu.VMEM((3, 1, knot_dev), F32),
+            pltpu.VMEM((5, source_dev), F32),
+            pltpu.VMEM((3, 1, knot_dev), F32),
         ),
-        in_specs=[hbm] * 7 + [smem] * 2,
-        out_specs=[vmem] * 4,
+        in_specs=[hbm] * 13,
+        out_specs=[vmem] * 8,
         scratch_shapes=[
             pltpu.VMEM(a.shape, a.dtype)
             for a in (
@@ -434,6 +462,8 @@
             )
         ]
         + [
+            pltpu.SMEM((buckets,), jnp.int32),
+            pltpu.SMEM((3,), F32),
             pltpu.VMEM((n_src, 8, 128), F32),
             pltpu.VMEM((n_tm, 2, cap), F32),
             pltpu.VMEM((n_tm, 2, cap), F32),
@@ -446,9 +476,9 @@
             pltpu.VMEM((n_src, 1, 128), F32),
             pltpu.VMEM((n_tm, 1, 128), F32),
             pltpu.VMEM((n_tm, 128, cap), BF16),
-            pltpu.VMEM((n_tm, 128, cap), BF16),
-            pltpu.VMEM((384, 128), F32),
-            pltpu.SemaphoreType.DMA((7,)),
+            pltpu.VMEM((n_tm, 256, cap), BF16),
+            pltpu.VMEM((n_tm, 9, 16, cap), BF16),
+            pltpu.SemaphoreType.DMA((13,)),
         ]
         + [pltpu.SemaphoreType.DMA((5,))] + [pltpu.SemaphoreType.DMA((2,))] * 7,
         compiler_params=pltpu.CompilerParams(collective_id=0, has_side_effects=True),
@@ -462,7 +492,12 @@
         knot_vector,
         bucket_fill.reshape(buckets),
         recurrence,
+        source_search,
+        knot_search,
+        source_solution,
+        knot_solution,
     )
+    held = [pltpu.with_memory_space_constraint(v, pltpu.VMEM) for v in held]
     outs = pl.pallas_call(
         finish,
         out_shape=(
@@ -475,9 +510,9 @@
             jax.ShapeDtypeStruct((3, 1, knot_dev), F32),
             jax.ShapeDtypeStruct((1, 4), F32),
         ),
-        in_specs=[vmem] * 8 + [smem],
+        in_specs=[vmem] * 8,
         out_specs=[vmem] * 8,
-    )(raw, sraw, kraw, scal, source_search, knot_search, source_solution, knot_solution, recurrence)
+    )(*held)
     return (*outs[:7], outs[7].reshape(4))
 
 

time: 56.7 us -> 53.5 us (0.944)
  Pallas kernels: 55.8 us -> 52.7 us
    pallas_call x1, Pallas kernels: 54.3 us -> 52 us  [shards(): pl.pallas_call(functools.partial(iterate, n_src, n_tm, total_obs, unknown...]
    pallas_call x1, Pallas kernels: 1.55 us -> 0.69 us  [shards(): pl.pallas_call(finish, out_shape=(jax.ShapeDtypeStruct((buckets, cap), F3...]
where the time goes in v3:
time: 53.5 us; the launch traced here: 53.3 us
  Pallas kernels  52.7 us (99%)
  between operations  0.65 us (1%)
    pallas_call x1, Pallas kernels, shards(): pl.pallas_call(functools.partial(iterate, n_src, n_tm, total_obs, unknown...  52 us

profile of v3, /device:TPU:1, one launch (start us, length us, event | category | flops | bytes accessed | tf_op | source)
XLA Modules:
  0.0 53.3 jit_solution(4625749627614724130)
XLA Ops:
  0.6 52.0 %shard_map.188 = (f32[8,256]{1,0:T(8,128)S(1)}, f32[5,1024]{1,0:T(8,128)S(1)}, f32[3,1,256]{2,1,0:T(1,128)S(1)}, f32[8,128]{1,0:T(8,128)S(1)}, f32[5,1024]{1,0:T...) custom-call(f32[8,256]{1,0:T(8,128)} %left_hbm.1, f32[5,8,256]{2,1,0:T(8,128)} %sc_hbm.1, ...), custom_call_target="tpu_custom_call" | custom-call | tf_op jit(solution)/shard_map/pallas_call | solution.py:438
  52.6 0.7 %shard_map.189 = (f32[8,256]{1,0:T(8,128)}, f32[5,1024]{1,0:T(8,128)}, f32[3,1,256]{2,1,0:T(1,128)}, f32[5,1024]{1,0:T(8,128)}, f32[3,1,256]{2,1,0:T(1,128)}, /*...) custom-call(f32[8,256]{1,0:T(8,128)S(1)} %get-tuple-element.24.raw_ref, ...), custom_call_target="tpu_custom_call" | custom-call | tf_op jit(solution)/shard_map/pallas_call | solution.py:501

commit v4 on v3

--- a/solution.py
+++ b/solution.py
@@ -8,6 +8,7 @@
 from jax.sharding import PartitionSpec as P
 
 N_X = 4
+FAR = 5
 EPSILON = 1e-06
 F32 = jnp.float32
 BF16 = jnp.bfloat16
@@ -69,6 +70,8 @@
     rrcv,
     rs_send,
     rs_recv,
+    legs,
+    joined,
     ar1a,
     ar1b,
     ar2a,
@@ -161,6 +164,8 @@
     for load in loads:
         load.start()
 
+    far = [d for d in range(8, FAR - 1, -1)] + [-d for d in range(7, FAR - 1, -1)]
+
     barrier = pltpu.get_barrier_semaphore()
     for dz, dx in near:
         pl.semaphore_signal(barrier, inc=1, device_id={"src": at(dz, dx)}, device_id_type=pl.DeviceIdType.MESH)
@@ -169,38 +174,10 @@
             barrier, inc=1, device_id={"tm": lax.rem(m + d, n_tm)}, device_id_type=pl.DeviceIdType.MESH
         )
 
-    for load in loads[:7]:
-        load.wait()
-
+    loads[0].wait()
     for a in range(3):
         for sub in range(2):
             ag[s, a * 2 + sub : a * 2 + sub + 1, :] = kv_ref[a, :, sub * 128 : (sub + 1) * 128]
-
-    alpha = rec_ref[0]
-    pad3 = jnp.zeros((3, 128), F32)
-    table = jnp.concatenate(
-        [jnp.concatenate([sv_ref[:, l * 128 : (l + 1) * 128], pad3], axis=0) for l in range(8)], axis=0
-    )
-    stable = jnp.concatenate(split3(table), axis=1)
-    rows128 = lax.broadcasted_iota(jnp.int32, (128, cap), 0)
-    lane = lax.broadcasted_iota(jnp.int32, (1, cap), 1)
-
-    for t in range(n_tm):
-        idx = si_ref[t : t + 1, :]
-        hi = jnp.bitwise_and(idx, 127)
-        lo = jnp.right_shift(idx, 7)
-        oh = jnp.where(rows128 == hi, 1.0, 0.0).astype(BF16)
-        ohs[t] = oh
-        found = lax.dot_general(
-            stable, jnp.concatenate([oh, oh, oh], axis=0), NN, preferred_element_type=F32
-        )
-        picked = jnp.zeros((8, cap), F32)
-        for l in range(8):
-            picked = picked + jnp.where(lo == l, found[l * 8 : (l + 1) * 8], 0.0)
-        coef = sc_ref[:, t, :]
-        image = jnp.sum(coef * picked[0:5], axis=0, keepdims=True)
-        pbuf[t, 0:1, :] = image - alpha * left_ref[t : t + 1, :]
-        pbuf[t, 1:2, :] = jnp.where(lane < fill_ref[t], 1.0, 0.0)
 
     pl.semaphore_wait(barrier, len(near) + n_tm - 1)
 
@@ -229,6 +206,35 @@
     for dz, dx in near:
         hand_on(ag.at[s, six], at(dz, dx), 1 if dz == 4 else 2 if dz == -4 else 3)
     pending.append(lambda: taken(n_src - 1, 0))
+    for load in loads[1:7]:
+        load.wait()
+
+    alpha = rec_ref[0]
+    pad3 = jnp.zeros((3, 128), F32)
+    table = jnp.concatenate(
+        [jnp.concatenate([sv_ref[:, l * 128 : (l + 1) * 128], pad3], axis=0) for l in range(8)], axis=0
+    )
+    stable = jnp.concatenate(split3(table), axis=1)
+    rows128 = lax.broadcasted_iota(jnp.int32, (128, cap), 0)
+    lane = lax.broadcasted_iota(jnp.int32, (1, cap), 1)
+
+    for t in range(n_tm):
+        idx = si_ref[t : t + 1, :]
+        hi = jnp.bitwise_and(idx, 127)
+        lo = jnp.right_shift(idx, 7)
+        oh = jnp.where(rows128 == hi, 1.0, 0.0).astype(BF16)
+        ohs[t] = oh
+        found = lax.dot_general(
+            stable, jnp.concatenate([oh, oh, oh], axis=0), NN, preferred_element_type=F32
+        )
+        picked = jnp.zeros((8, cap), F32)
+        for l in range(8):
+            picked = picked + jnp.where(lo == l, found[l * 8 : (l + 1) * 8], 0.0)
+        coef = sc_ref[:, t, :]
+        image = jnp.sum(coef * picked[0:5], axis=0, keepdims=True)
+        pbuf[t, 0:1, :] = image - alpha * left_ref[t : t + 1, :]
+        pbuf[t, 1:2, :] = jnp.where(lane < fill_ref[t], 1.0, 0.0)
+
     tm_send(lambda o: pbuf.at[o], prcv.at[m], pbuf.at[tm_rest], p_sem)
     prcv[m] = pbuf[m]
     for which, sign, reach in ((1, 1, 4), (2, -1, 3)):
@@ -239,6 +245,9 @@
 
     for load in loads[7:]:
         load.wait()
+
+    for dz in far:
+        rs_recv[pl.ds(at(dz, 0) - x, N_X)] = jnp.zeros((N_X, 8, 128), F32)
 
     rows256 = lax.broadcasted_iota(jnp.int32, (256, cap), 0)
     for i in range(n_tm):
@@ -302,7 +311,44 @@
         for half in range(2):
             rs_send[:, a * 2 + half, :] = turned[half * 64 : (half + 1) * 64]
 
-    src_send(lambda o: rs_send.at[o, six], rs_recv.at[s, six], rs_send.at[src_rest, six], rs_sem)
+    def add_up(block, target, slot, which):
+        pltpu.make_async_remote_copy(
+            src_ref=block,
+            dst_ref=slot,
+            send_sem=rs_sem.at[0],
+            recv_sem=rs_sem.at[which],
+            device_id={"src": target},
+            device_id_type=pl.DeviceIdType.MESH,
+        ).start()
+
+    for n, dz in enumerate(far):
+        short = 4 if dz > 0 else -4
+        plane = pl.ds(at(dz, 0) - x, N_X)
+        add_up(rs_send.at[plane, six], at(dz - short, 0), legs.at[n, :, six], 2)
+    for dz in [sign * d for d in range(FAR - 1, 0, -1) for sign in (1, -1) if d != 4] + [0]:
+        for dx in (2, 1, 3, 0):
+            if dz or dx:
+                add_up(rs_send.at[at(dz, dx), six], at(dz, dx), rs_recv.at[s, six], 1)
+    pending.append(lambda: arrived("src", rs_send.at[src_rest, six], rs_sem, 0))
+    whole = legs.at[:, :, six]
+    pltpu.make_async_remote_copy(
+        src_ref=whole,
+        dst_ref=whole,
+        send_sem=rs_sem.at[0],
+        recv_sem=rs_sem.at[2],
+        device_id={"src": s},
+        device_id_type=pl.DeviceIdType.MESH,
+    ).wait_recv()
+    for n, sign in enumerate((1, -1)):
+        added = rs_send[pl.ds(at(4 * sign, 0) - x, N_X)]
+        for leg, dz in enumerate(far):
+            if dz * sign > 0:
+                added = added + legs[leg]
+        joined[n] = added
+    for dx in (2, 1, 3, 0):
+        for n, sign in enumerate((1, -1)):
+            target = at(4 * sign, dx)
+            add_up(joined.at[n, lax.rem(x + dx, N_X), six], target, rs_recv.at[s, six], 1)
     rs_recv[s] = rs_send[s]
     arrived("tm", rrcv.at[tm_rest], r_sem, 1)
 
@@ -337,7 +383,7 @@
         sraw_out[:, l * 128 : (l + 1) * 128] = own
         squares = squares + jnp.sum(own * own, axis=0, keepdims=True)
 
-    arrived("src", rs_recv.at[src_rest, six], rs_sem, 1)
+    arrived("src", rs_recv.at[pl.ds(0, n_src - 1 - N_X * len(far)), six], rs_sem, 1)
     gathered = jnp.sum(rs_recv[...], axis=0)
     for a in range(3):
         for sub in range(2):
@@ -471,6 +517,8 @@
             pltpu.VMEM((n_tm, 1, cap), F32),
             pltpu.VMEM((n_src, 8, 128), F32),
             pltpu.VMEM((n_src, 8, 128), F32),
+            pltpu.VMEM((17 - 2 * FAR, N_X, 8, 128), F32),
+            pltpu.VMEM((2, N_X, 8, 128), F32),
             pltpu.VMEM((n_src, 1, 128), F32),
             pltpu.VMEM((n_tm, 1, 128), F32),
             pltpu.VMEM((n_src, 1, 128), F32),
@@ -480,7 +528,8 @@
             pltpu.VMEM((n_tm, 9, 16, cap), BF16),
             pltpu.SemaphoreType.DMA((13,)),
         ]
-        + [pltpu.SemaphoreType.DMA((5,))] + [pltpu.SemaphoreType.DMA((2,))] * 7,
+        + [pltpu.SemaphoreType.DMA((5,))]
+        + [pltpu.SemaphoreType.DMA((3,))] * 7,
         compiler_params=pltpu.CompilerParams(collective_id=0, has_side_effects=True),
     )(
         left_vector,

time: 53.5 us -> 52.7 us (0.985)
  Pallas kernels: 52.7 us -> 51.9 us
    pallas_call x1, Pallas kernels: 52 us -> 51.2 us  [shards(): pl.pallas_call(functools.partial(iterate, n_src, n_tm, total_obs, unknown...]
where the time goes in v4:
time: 52.7 us; the launch traced here: 52.5 us
  Pallas kernels  51.9 us (98%)
  between operations  0.65 us (1%)
    pallas_call x1, Pallas kernels, shards(): pl.pallas_call(functools.partial(iterate, n_src, n_tm, total_obs, unknown...  51.2 us

profile of v4, /device:TPU:1, one launch (start us, length us, event | category | flops | bytes accessed | tf_op | source)
XLA Modules:
  0.0 52.5 jit_solution(7199854665455647513)
XLA Ops:
  0.6 51.2 %shard_map.188 = (f32[8,256]{1,0:T(8,128)S(1)}, f32[5,1024]{1,0:T(8,128)S(1)}, f32[3,1,256]{2,1,0:T(1,128)S(1)}, f32[8,128]{1,0:T(8,128)S(1)}, f32[5,1024]{1,0:T...) custom-call(f32[8,256]{1,0:T(8,128)} %left_hbm.1, f32[5,8,256]{2,1,0:T(8,128)} %sc_hbm.1, ...), custom_call_target="tpu_custom_call" | custom-call | tf_op jit(solution)/shard_map/pallas_call | solution.py:484
  51.9 0.7 %shard_map.189 = (f32[8,256]{1,0:T(8,128)}, f32[5,1024]{1,0:T(8,128)}, f32[3,1,256]{2,1,0:T(1,128)}, f32[5,1024]{1,0:T(8,128)}, f32[3,1,256]{2,1,0:T(1,128)}, /*...) custom-call(f32[8,256]{1,0:T(8,128)S(1)} %get-tuple-element.24.raw_ref, ...), custom_call_target="tpu_custom_call" | custom-call | tf_op jit(solution)/shard_map/pallas_call | solution.py:550

commit v5 on v4

--- a/solution.py
+++ b/solution.py
@@ -132,8 +132,35 @@
         send_all("tm", tm_order, m, n_tm, src, dst, sems)
         pending.append(lambda: arrived("tm", whole, sems, 0))
 
+    plane_size = N_X * n_tm
+    spot = x * n_tm + m
+    plane_peers = [(dx, dm) for dx in (2, 1, 3, 0) for dm in (4, 3, 5, 2, 6, 7, 1, 0) if dx or dm]
+    line_peers = [n_z // 2] + [sign * d for d in range(n_z // 2 - 1, 0, -1) for sign in (1, -1)]
+
+    def tell(row, target, sems):
+        pltpu.make_async_remote_copy(
+            src_ref=row,
+            dst_ref=row,
+            send_sem=sems.at[0],
+            recv_sem=sems.at[1],
+            device_id=target,
+            device_id_type=pl.DeviceIdType.MESH,
+        ).start()
+
+    def plane_send(buf, sems):
+        for dx, dm in plane_peers:
+            tell(buf.at[spot], {"src": z * N_X + lax.rem(x + dx, N_X), "tm": lax.rem(m + dm, n_tm)}, sems)
+        pending.append(lambda: arrived("src", buf.at[pl.ds(0, plane_size - 1)], sems, 0))
+
+    def line_send(buf, sems):
+        for dz in line_peers:
+            tell(buf.at[z], {"src": lax.rem(z + dz + n_z, n_z) * N_X + x}, sems)
+        pending.append(lambda: arrived("src", buf.at[pl.ds(0, n_z - 1)], sems, 0))
+
     src_rest = pl.ds(0, n_src - 1)
     tm_rest = pl.ds(0, n_tm - 1)
+    plane_rest = pl.ds(0, plane_size - 1)
+    line_rest = pl.ds(0, n_z - 1)
     six = pl.ds(0, 6)
 
     def at(dz, dx):
@@ -392,14 +419,14 @@
             kraw_out[a, :, sub * 128 : (sub + 1) * 128] = own
             squares = squares + own * own
 
-    ar2b[m] = squares
-    tm_send(lambda o: ar2b.at[m], ar2b.at[m], ar2b.at[tm_rest], ar2b_sem)
-    arrived("tm", ar2b.at[tm_rest], ar2b_sem, 1)
-    ar2a[s] = jnp.sum(ar2b[...], axis=0)
-    src_send(lambda o: ar2a.at[s], ar2a.at[s], ar2a.at[src_rest], ar2a_sem)
-    arrived("src", ar2a.at[src_rest], ar2a_sem, 1)
+    ar2a[spot] = squares
+    plane_send(ar2a, ar2a_sem)
+    arrived("src", ar2a.at[plane_rest], ar2a_sem, 1)
+    ar2b[z] = jnp.sum(ar2a[...], axis=0)
+    line_send(ar2b, ar2b_sem)
+    arrived("src", ar2b.at[line_rest], ar2b_sem, 1)
     alpha_next = jnp.sqrt(
-        jnp.sum(jnp.sum(ar2a[...], axis=0), axis=1, keepdims=True) / unknowns + EPSILON
+        jnp.sum(jnp.sum(ar2b[...], axis=0), axis=1, keepdims=True) / unknowns + EPSILON
     )
     pivot = rec_ref[1]
     remainder = rec_ref[2]
@@ -521,8 +548,8 @@
             pltpu.VMEM((2, N_X, 8, 128), F32),
             pltpu.VMEM((n_src, 1, 128), F32),
             pltpu.VMEM((n_tm, 1, 128), F32),
-            pltpu.VMEM((n_src, 1, 128), F32),
-            pltpu.VMEM((n_tm, 1, 128), F32),
+            pltpu.VMEM((N_X * n_tm, 1, 128), F32),
+            pltpu.VMEM((n_src // N_X, 1, 128), F32),
             pltpu.VMEM((n_tm, 128, cap), BF16),
             pltpu.VMEM((n_tm, 256, cap), BF16),
             pltpu.VMEM((n_tm, 9, 16, cap), BF16),

time: 52.7 us -> 52.6 us (level)
  no operation moved by 1% of the time
where the time goes in v5:
time: 52.6 us; the launch traced here: 52.5 us
  Pallas kernels  51.8 us (98%)
  between operations  0.65 us (1%)
    pallas_call x1, Pallas kernels, shards(): pl.pallas_call(functools.partial(iterate, n_src, n_tm, total_obs, unknown...  51.2 us

profile of v5, /device:TPU:1, one launch (start us, length us, event | category | flops | bytes accessed | tf_op | source)
XLA Modules:
  0.0 52.5 jit_solution(18430525780059107406)
XLA Ops:
  0.6 51.2 %shard_map.188 = (f32[8,256]{1,0:T(8,128)S(1)}, f32[5,1024]{1,0:T(8,128)S(1)}, f32[3,1,256]{2,1,0:T(1,128)S(1)}, f32[8,128]{1,0:T(8,128)S(1)}, f32[5,1024]{1,0:T...) custom-call(f32[8,256]{1,0:T(8,128)} %left_hbm.1, f32[5,8,256]{2,1,0:T(8,128)} %sc_hbm.1, ...), custom_call_target="tpu_custom_call" | custom-call | tf_op jit(solution)/shard_map/pallas_call | solution.py:511
  51.8 0.7 %shard_map.189 = (f32[8,256]{1,0:T(8,128)}, f32[5,1024]{1,0:T(8,128)}, f32[3,1,256]{2,1,0:T(1,128)}, f32[5,1024]{1,0:T(8,128)}, f32[3,1,256]{2,1,0:T(1,128)}, /*...) custom-call(f32[8,256]{1,0:T(8,128)S(1)} %get-tuple-element.24.raw_ref, ...), custom_call_target="tpu_custom_call" | custom-call | tf_op jit(solution)/shard_map/pallas_call | solution.py:577
